TPU v7x, 32 devices: a whole 2x2x4 slice. The times are simulated.
32 devices in a mesh: dp: 4 (over z), tensor: 8 (over y, x, core).
Axes of the slice: x: 2, y: 2, z: 4, core: 2. Of those that a mesh axis runs over, the one named last changes fastest.
Arguments:
- hidden_in: bfloat16 [4, 1024, 2304], P('dp', 'tensor'), may hold values from -6 to 6
- prompt_len: int32 [4], P('dp'), may hold values from 1 to 1024, 2560 in all
- start_pos: int32 [4], P('dp'), may hold values from 0 to 511
- routes: int32 [4, 1024, 2], P('dp'), may hold values from 0 to 7, as said below
- trainer_qkv: float32 [2304, 3, 2048], P(('tensor', 'dp')), may hold values from -1 to 1
- trainer_out: float32 [2048, 2304], P(('tensor', 'dp')), may hold values from -0.125 to 0.125
- trainer_gate: float32 [2304, 5760], P('tensor'), may hold values from -0.125 to 0.125
- trainer_up: float32 [2304, 5760], P('tensor'), may hold values from -0.125 to 0.125
- trainer_down: float32 [2304, 5760], P('tensor'), may hold values from -0.078125 to 0.078125
- attn_gain: float32 [2304], replicated, may hold values from 0.25 to 1.75
- moe_gain: float32 [2304], replicated, may hold values from 0.25 to 1.75
- router: bfloat16 [2304, 8], replicated, may hold values from -0.125 to 0.125
Outputs:
- server_qkv: bfloat16 [2304, 3, 2048], P(None, None, 'tensor')
- server_out: bfloat16 [2048, 2304], P('tensor')
- server_gate: bfloat16 [2304, 5760], P(None, 'tensor')
- server_up: bfloat16 [2304, 5760], P(None, 'tensor')
- server_down: bfloat16 [2304, 5760], P(None, 'tensor')
- hidden_out: bfloat16 [4, 1024, 2304], P('dp', 'tensor')
- kv_cache: bfloat16 [4, 2, 1024, 2048], P('dp', None, None, 'tensor')
Inputs may be any that keep to these rules, and one draw needn't show every extreme that they name: `routes`: each row names two different experts; expert 0 is named by at most 512 rows of each prompt and by exactly 512 rows of some prompt.
All inputs are finite; a program needn't handle non-finite values. No bound on the sum of `prompt_len` on one device may be relied on, other than what follows from the above.
Results may differ from a plain program's by a relative error of at most 0.011.
The roundings to bfloat16 on the way count: a program that leaves them out, or rounds other values in their place, can miss the bound.
Values may be sent and summed in bfloat16 or wider, within the bound.
No kernel may reach another device: no remote copies, remote signals or barrier semaphores. Data moves between devices by JAX's collectives and lax.ppermute only.
A program may use at most 256 MiB of HBM per device.

v0:
```python
import jax
import jax.numpy as jnp
from jax import lax
from jax.sharding import PartitionSpec as P

HEAD_DIM = 64


def rms_scale(values, gain_row):
    mean_sq = jnp.mean(values * values, axis=-1, keepdims=True)
    return values * lax.rsqrt(mean_sq + 1e-05) * gain_row


def rotate(head_block, positions):
    half_dim = head_block.shape[-1] // 2
    inv_freq = jnp.power(
        10000.0, jnp.arange(half_dim, dtype=jnp.float32) * (-2.0 / head_block.shape[-1])
    )
    angles = positions.astype(jnp.float32)[:, None] * inv_freq[None, :]
    cosine = jnp.cos(angles)[:, None, :]
    sine_part = jnp.sin(angles)[:, None, :]
    first_half = head_block[..., :half_dim]
    second_half = head_block[..., half_dim:]
    return jnp.concatenate(
        [
            first_half * cosine - second_half * sine_part,
            second_half * cosine + first_half * sine_part,
        ],
        axis=-1,
    )


def attend_block(query_blk, key_blk, value_blk, row_start):
    scores = jnp.einsum(
        "qhd,khd->hqk", query_blk, key_blk, preferred_element_type=jnp.float32
    ) * query_blk.shape[-1] ** (-0.5)
    row_ids = row_start + jnp.arange(query_blk.shape[0], dtype=jnp.int32)
    col_ids = jnp.arange(key_blk.shape[0], dtype=jnp.int32)
    scores = jnp.where(row_ids[None, :, None] >= col_ids[None, None, :], scores, -1e30)
    row_max = jnp.max(scores, axis=-1, keepdims=True)
    exp_scores = jnp.exp(scores - row_max)
    attn_probs = (exp_scores / jnp.sum(exp_scores, axis=-1, keepdims=True)).astype(jnp.bfloat16)
    return jnp.einsum(
        "hqk,khd->qhd", attn_probs, value_blk, preferred_element_type=jnp.float32
    ).astype(jnp.bfloat16)


def shards(
    hidden_in,
    prompt_len,
    start_pos,
    routes,
    trainer_qkv,
    trainer_out,
    trainer_gate,
    trainer_up,
    trainer_down,
    attn_gain,
    moe_gain,
    router,
):
    tensor_size = lax.axis_size("tensor")
    replica_count = lax.axis_size("dp")
    expert_mats = (
        lax.all_to_all(
            trainer_gate.astype(jnp.bfloat16), "tensor", split_axis=1, concat_axis=0, tiled=True
        ),
        lax.all_to_all(
            trainer_up.astype(jnp.bfloat16), "tensor", split_axis=1, concat_axis=0, tiled=True
        ),
        lax.all_to_all(
            trainer_down.astype(jnp.bfloat16), "tensor", split_axis=1, concat_axis=0, tiled=True
        ),
    )
    server_gate, server_up, server_down = expert_mats
    qkv_cast = trainer_qkv.astype(jnp.bfloat16)
    out_cast = trainer_out.astype(jnp.bfloat16)
    column_part = lax.all_to_all(qkv_cast, "tensor", split_axis=2, concat_axis=0, tiled=True)
    stacked, server_out = (
        lax.all_gather(column_part, "dp", axis=0, tiled=True),
        lax.all_gather(out_cast, "dp", axis=0, tiled=True),
    )
    block_rows = stacked.shape[0] // (replica_count * tensor_size)
    server_qkv = (
        stacked.reshape(replica_count, tensor_size, block_rows, 3, stacked.shape[2])
        .transpose(1, 0, 2, 3, 4)
        .reshape(stacked.shape)
    )
    rows_dev = hidden_in.shape[1]
    seq_len = rows_dev * tensor_size
    length = prompt_len[0]
    offset = start_pos[0]
    my_first = lax.axis_index("tensor") * rows_dev
    tokens = hidden_in[0].astype(jnp.float32)
    normed = rms_scale(tokens, attn_gain).astype(jnp.bfloat16)
    local_width = server_qkv.shape[2]
    heads_here = local_width // HEAD_DIM
    piece = lax.all_gather(normed, "tensor", axis=0, tiled=True)
    mixed = jnp.einsum("sd,dtc->stc", piece, server_qkv, preferred_element_type=jnp.float32)
    places = offset + jnp.arange(piece.shape[0], dtype=jnp.int32)
    query_rot = rotate(mixed[:, 0].reshape(-1, heads_here, HEAD_DIM), places).reshape(
        -1, local_width
    )
    key_rot = rotate(mixed[:, 1].reshape(-1, heads_here, HEAD_DIM), places).reshape(-1, local_width)
    qkv_rows = jnp.stack([query_rot, key_rot, mixed[:, 2]], axis=1).astype(jnp.bfloat16)
    query_all = qkv_rows[:, 0].reshape(seq_len, heads_here, HEAD_DIM)
    keys_all = qkv_rows[:, 1].reshape(seq_len, heads_here, HEAD_DIM)
    values_all = qkv_rows[:, 2].reshape(seq_len, heads_here, HEAD_DIM)
    block_len = min(512, seq_len)
    block_outs = []
    for block_id in range(seq_len // block_len):
        row_lo = block_id * block_len
        row_hi = row_lo + block_len
        query_blk = query_all[row_lo:row_hi]
        key_blk = keys_all[:row_hi]
        value_blk = values_all[:row_hi]
        block_result = attend_block(query_blk, key_blk, value_blk, row_lo)
        block_outs.append(block_result)
    attended = jnp.concatenate(block_outs, axis=0).reshape(seq_len, local_width)
    attn_sum = lax.psum_scatter(
        jnp.dot(attended, server_out, preferred_element_type=jnp.float32).astype(jnp.bfloat16),
        "tensor",
        scatter_dimension=0,
        tiled=True,
    ).astype(jnp.float32)
    middle = (tokens + attn_sum).astype(jnp.bfloat16)
    normed_moe = rms_scale(middle.astype(jnp.float32), moe_gain).astype(jnp.bfloat16)
    local_routes = lax.dynamic_slice_in_dim(routes[0], my_first, rows_dev, 0)
    local_valid = my_first + jnp.arange(rows_dev, dtype=jnp.int32) < length
    logits = jnp.dot(normed_moe, router, preferred_element_type=jnp.float32)
    expert_ids = jnp.arange(router.shape[1], dtype=jnp.int32)
    logit_first = jnp.sum(
        jnp.where(local_routes[:, 0:1] == expert_ids[None, :], logits, 0.0), axis=1
    )
    logit_second = jnp.sum(
        jnp.where(local_routes[:, 1:2] == expert_ids[None, :], logits, 0.0), axis=1
    )
    other_logit = jnp.where(local_routes[:, 0] == 0, logit_second, logit_first)
    local_routed = jnp.any(local_routes == 0, axis=1)
    route_w = jnp.where(local_routed, jax.nn.sigmoid(logits[:, 0] - other_logit), 0.0)
    gathered = lax.all_gather(normed_moe, "tensor", axis=0, tiled=True)
    seq_ids = jnp.arange(seq_len, dtype=jnp.int32)
    all_routed = jnp.any(routes[0] == 0, axis=1)
    capacity = seq_len // 2
    slot = jnp.cumsum(all_routed.astype(jnp.int32)) - 1
    slot_rows = (
        jnp.full((capacity,), seq_len, jnp.int32)
        .at[jnp.where(all_routed, slot, capacity)]
        .set(seq_ids, mode="drop")
    )
    picked = gathered[jnp.minimum(slot_rows, seq_len - 1)]
    gate_val = jnp.dot(picked, server_gate, preferred_element_type=jnp.float32)
    up_val = jnp.dot(picked, server_up, preferred_element_type=jnp.float32)
    act = (jax.nn.silu(gate_val) * up_val).astype(jnp.bfloat16)
    slot_sums = lax.dot_general(
        act, server_down, (((1,), (1,)), ((), ())), preferred_element_type=jnp.float32
    )
    terms = (
        jnp.zeros((seq_len, normed_moe.shape[1]), jnp.float32)
        .at[slot_rows]
        .add(slot_sums, mode="drop")
    )
    expert_sum = lax.psum_scatter(
        terms.astype(jnp.bfloat16), "tensor", scatter_dimension=0, tiled=True
    ).astype(jnp.float32)
    result = middle.astype(jnp.float32) + route_w[:, None] * expert_sum
    hidden_out = jnp.where(local_valid[:, None], result, 0.0).astype(jnp.bfloat16)[None]
    seq_valid = jnp.arange(seq_len, dtype=jnp.int32) < length
    cache_pair = jnp.where(
        seq_valid[None, :, None], qkv_rows[:, 1:3].transpose(1, 0, 2), jnp.zeros((), jnp.bfloat16)
    )
    return (
        server_qkv,
        server_out,
        server_gate,
        server_up,
        server_down,
        hidden_out,
        cache_pair[None],
    )


def solution(mesh):
    placed = (
        P("dp", "tensor", None),
        P("dp"),
        P("dp"),
        P("dp", None, None),
        P(("tensor", "dp"), None, None),
        P(("tensor", "dp"), None),
        P("tensor", None),
        P("tensor", None),
        P("tensor", None),
        P(),
        P(),
        P(),
    )
    return jax.shard_map(
        shards,
        mesh=mesh,
        in_specs=placed,
        out_specs=(
            P(None, None, "tensor"),
            P("tensor", None),
            P(None, "tensor"),
            P(None, "tensor"),
            P(None, "tensor"),
            P("dp", "tensor", None),
            P("dp", None, None, "tensor"),
        ),
        check_vma=False,
    )
```

profile of v0, /device:TPU:0, one launch (start us, length us, event | category | flops | bytes accessed | tf_op | source)
XLA Modules:
  0.0 508.5 jit_solution(11771919291552511364)
XLA Ops:
  16.3 18.9 %all_to_all.75 = bf16[8,2,27648]{2,1,0:T(2,128)(2,1)} all-to-all(bf16[8,2,27648]{2,1,0:T(2,128)(2,1)} %reshape.272), channel_id=1, replica_groups=mesh['dp'=4,'tensor'=8] {'tensor'}, dimensions={0} | all-to-all | bytes 1769472 | tf_op jit(solution)/shard_map/all_to_all | solution.py:78
  46.1 65.7 %all-gather.5.cloned.1.call-done = bf16[2304,3,256]{2,0,1:T(8,128)(2,1)} async-done(((bf16[576,3,256]{2,0,1:T(8,128)(2,1)}), bf16[2304,3,256]{2,0,1:T(8,128)(2,1)}) %all-gather.5.cloned.1.call-update) | async-done | bytes 3538960 | tf_op jit(solution)/shard_map/all_gather | solution.py:80
  115.9 35.8 %all-gather.9.cloned.1.call-done = bf16[1024,2304]{1,0:T(8,128)(2,1)} async-done(((bf16[128,2304]{1,0:T(8,128)(2,1)}), bf16[1024,2304]{1,0:T(8,128)(2,1)}) %all-gather.9.cloned.1.call-update) | async-done | bytes 4718608 | tf_op jit(solution)/shard_map/all_gather | solution.py:98
  151.8 6.8 %fusion.61 = (bf16[1024,3,256]{0,2,1:T(8,128)(2,1)S(1)}, f32[1024,3,256]{0,2,1:T(8,128)S(1)}) fusion(bf16[2304,3,256]{2,0,1:T(8,128)(2,1)} %bitcast.102, bf16[1024,2304]{1,0:T(8,128)(2,1)} %all-gather.9.cloned.1.call-done), kind=kOutput, calls=%fused_computation.108 | convolution fusion | flops 3624665088 | bytes 12976128 | tf_op jit(solution)/shard_map/sd,dtc->stc/dot_general | solution.py:99
  159.2 5.4 %fusion.62 = (f32[4,512]{1,0:T(4,128)S(1)}, f32[4,512,1024]{2,1,0:T(8,128)}) fusion(pred[512,1024]{1,0:T(8,128)(4,1)S(1)} %iota_compare_fusion, bf16[1024,4,32]{0,2,1:T(8,128)(2,1)S(1)} %get-tuple-element.52, bf16[1024,4,32]{0,2,1:T(8,128)(2,1)S(1)} %get-tuple-element.53, bf16[1024,4,32]{0,2,1:T(8,128)(2,1)S(1)} %get-tuple-element.49, ...), kind=kOutput, calls=%fused_computation.109 | convolution fusion | flops 278397952 | bytes 9969664 | tf_op jit(solution)/shard_map/sub | solution.py:41
  174.5 10.0 %all-gather.7.cloned.1.call-done = bf16[256,2304]{1,0:T(8,128)(2,1)} async-done(((bf16[64,2304]{1,0:T(8,128)(2,1)}), bf16[256,2304]{1,0:T(8,128)(2,1)}) %all-gather.7.cloned.1.call-update) | async-done | bytes 1179664 | tf_op jit(solution)/shard_map/all_gather | solution.py:81
  189.9 52.6 %reduce-scatter.3.cloned.1.call-done = bf16[128,2304]{1,0:T(8,128)(2,1)} async-done(((bf16[1024,2304]{1,0:T(8,128)(2,1)}), bf16[128,2304]{1,0:T(8,128)(2,1)}) %reduce-scatter.3.cloned.1.call-update) | async-done | bytes 589840 | tf_op jit(solution)/shard_map/reduce_scatter | solution.py:120
  246.0 4.9 convert_element_type.88
  250.9 8.5 %all_to_all.59 = bf16[288,8,720]{2,1,0:T(8,128)(2,1)} reshape(bf16[288,5760]{1,0:T(8,128)(2,1)} %convert_element_type.88) | data formatting | bytes 6635520 | tf_op jit(solution)/shard_map/all_to_all | solution.py:65
  268.4 5.0 convert_element_type.89
  273.4 8.5 %all_to_all.63 = bf16[288,8,720]{2,1,0:T(8,128)(2,1)} reshape(bf16[288,5760]{1,0:T(8,128)(2,1)} %convert_element_type.89) | data formatting | bytes 6635520 | tf_op jit(solution)/shard_map/all_to_all | solution.py:68
  286.4 35.8 %all-to-all-done.1 = bf16[288,8,720]{2,0,1:T(8,128)(2,1)} async-done(((bf16[288,8,720]{2,0,1:T(8,128)(2,1)}), bf16[288,8,720]{2,0,1:T(8,128)(2,1)}, u32[]{:S(2)}, u32[]{:S(2)}) %all-to-all-start.1) | async-done | bytes 3317792 | tf_op jit(solution)/shard_map/all_to_all | solution.py:65
  331.6 8.4 %all_to_all.67 = bf16[288,8,720]{2,1,0:T(8,128)(2,1)} reshape(bf16[288,5760]{1,0:T(8,128)(2,1)} %convert_element_type.90) | data formatting | bytes 6635520 | tf_op jit(solution)/shard_map/all_to_all | solution.py:71
  344.6 24.2 %all-to-all-done.2 = bf16[288,8,720]{2,0,1:T(8,128)(2,1)} async-done(((bf16[288,8,720]{2,0,1:T(8,128)(2,1)}), bf16[288,8,720]{2,0,1:T(8,128)(2,1)}, u32[]{:S(2)}, u32[]{:S(2)}) %all-to-all-start.2) | async-done | bytes 3317792 | tf_op jit(solution)/shard_map/all_to_all | solution.py:68
  378.5 7.8 %gather_fusion = bf16[512,2304]{1,0:T(8,128)(2,1)S(1)} fusion(bf16[1024,2304]{1,0:T(8,128)(2,1)} %all-gather.11.cloned.1.call-done, s32[1024]{0:T(1024)S(1)} %pad_clamp_fusion), kind=kCustom, calls=%fused_computation | custom fusion | bytes 4720640 | tf_op jit(solution)/shard_map/gather | solution.py:151
  386.4 5.0 fusion.72
  391.4 24.0 %all-to-all-done.3 = bf16[288,8,720]{2,0,1:T(8,128)(2,1)} async-done(((bf16[288,8,720]{2,0,1:T(8,128)(2,1)}), bf16[288,8,720]{2,0,1:T(8,128)(2,1)}, u32[]{:S(2)}, u32[]{:S(2)}) %all-to-all-start.3) | async-done | bytes 3317792 | tf_op jit(solution)/shard_map/all_to_all | solution.py:71
  415.4 9.9 %fusion.32 = f32[512,2304]{1,0:T(8,128)} fusion(bf16[2304,720]{1,0:T(8,128)(2,1)} %bitcast.12, f32[512,720]{0,1:T(8,128)} %fusion.72, bf16[512,2304]{1,0:T(8,128)(2,1)S(1)} %gather_fusion, bf16[2304,720]{1,0:T(8,128)(2,1)} %bitcast.10), kind=kOutput, calls=%fused_computation.51 | convolution fusion | flops 3399598080 | bytes 15187968 | tf_op jit(solution)/shard_map/dot_general | solution.py:155
  425.3 13.3 %scatter_custom_fusion.1 = f32[1024,2304]{1,0:T(8,128)} fusion(s32[512]{0:T(512)S(1)} %get-tuple-element.57, f32[512,2304]{1,0:T(8,128)} %fusion.32, f32[]{:T(128)} %constant.20.clone.1), kind=kCustom, calls=%fused_computation.12 | custom fusion | flops 1179648 | bytes 9437696 | tf_op jit(solution)/shard_map/scatter-add | solution.py:161
  438.6 6.4 %convert_element_type.109 = bf16[1024,2304]{1,0:T(8,128)(2,1)} convert(f32[1024,2304]{1,0:T(8,128)} %scatter_custom_fusion.1) | non-fusion elementwise | flops 2359296 | bytes 14155776 | tf_op jit(solution)/shard_map/convert_element_type | solution.py:164
  445.7 5.7 %copy.68 = bf16[2304,720]{0,1:T(8,128)(2,1)} copy(bf16[2304,720]{1,0:T(8,128)(2,1)} %bitcast.8) | data formatting | bytes 6635520
  451.4 5.9 %copy.69 = bf16[2304,720]{0,1:T(8,128)(2,1)} copy(bf16[2304,720]{1,0:T(8,128)(2,1)} %bitcast.10) | data formatting | bytes 6635520
  457.3 5.7 %copy.70 = bf16[2304,720]{0,1:T(8,128)(2,1)} copy(bf16[2304,720]{1,0:T(8,128)(2,1)} %bitcast.12) | data formatting | bytes 6635520
  466.8 31.4 %reduce-scatter.5.cloned.1.call-done = bf16[128,2304]{1,0:T(8,128)(2,1)} async-done(((bf16[1024,2304]{1,0:T(8,128)(2,1)}), bf16[128,2304]{1,0:T(8,128)(2,1)}) %reduce-scatter.5.cloned.1.call-update) | async-done | bytes 589840 | tf_op jit(solution)/shard_map/reduce_scatter | solution.py:163
  (99 shorter events, 86.9 us)
Async XLA Ops:
  7.2 459.3 %copy-start = (bf16[2304,8]{0,1:T(8,128)(2,1)S(1)}, bf16[2304,8]{0,1:T(8,128)(2,1)}, u32[]{:S(2)}) copy-start(bf16[2304,8]{0,1:T(8,128)(2,1)} %param.23) | copy-start | bytes 110596
  7.2 104.6 %all-gather.5.cloned.1.call-start = ((), (), s32[]{:S(2)}) async-start(), calls=%async_computation.6 | async-start | bytes 4423680 | tf_op jit(solution)/shard_map/all_gather | solution.py:80
  35.2 6.8 %copy-start.1 = (bf16[1,128,2304]{2,1,0:T(8,128)(2,1)S(1)}, bf16[1,128,2304]{2,1,0:T(8,128)(2,1)}, u32[]{:S(2)}) copy-start(bf16[1,128,2304]{2,1,0:T(8,128)(2,1)} %param.12) | copy-start | bytes 1769476
  35.2 7.0 %copy-start.10 = (f32[2304]{0:T(1024)S(1)}, f32[2304]{0:T(1024)}, u32[]{:S(2)}) copy-start(f32[2304]{0:T(1024)} %param.21) | copy-start | bytes 27652
  39.7 3.6 copy-start.9
  41.9 109.9 %all-gather.9.cloned.1.call-start = ((), (), s32[]{:S(2)}) async-start(), calls=%async_computation.8 | async-start | bytes 5308416 | tf_op jit(solution)/shard_map/all_gather | solution.py:98
  43.2 141.2 %all-gather.7.cloned.1.call-start = ((), (), s32[]{:S(2)}) async-start(), calls=%async_computation.7 | async-start | bytes 1474560 | tf_op jit(solution)/shard_map/all_gather | solution.py:81
  44.1 198.4 %reduce-scatter.3.cloned.1.call-start = ((), (), s32[]{:S(2)}) async-start(), calls=%async_computation.9 | async-start | bytes 5308416 | tf_op jit(solution)/shard_map/reduce_scatter | solution.py:120
  159.2 5.4 %copy-start.5 = (bf16[1024,4,32]{0,2,1:T(8,128)(2,1)}, bf16[1024,4,32]{0,2,1:T(8,128)(2,1)S(1)}, u32[]{:S(2)}) copy-start(bf16[1024,4,32]{0,2,1:T(8,128)(2,1)S(1)} %get-tuple-element.48) | copy-start | bytes 786436
  159.2 5.4 %copy-start.7 = (bf16[1024,4,32]{0,2,1:T(8,128)(2,1)}, bf16[1024,4,32]{0,2,1:T(8,128)(2,1)S(1)}, u32[]{:S(2)}) copy-start(bf16[1024,4,32]{0,2,1:T(8,128)(2,1)S(1)} %get-tuple-element.49) | copy-start | bytes 786436
  168.2 4.7 copy-start.13
  189.3 54.5 %copy-start.11 = (f32[2304]{0:T(1024)S(1)}, f32[2304]{0:T(1024)}, u32[]{:S(2)}) copy-start(f32[2304]{0:T(1024)} %param.22) | copy-start | bytes 27652
  189.3 189.2 %all-gather.11.cloned.1.call-start = ((), (), s32[]{:S(2)}) async-start(), calls=%async_computation.10 | async-start | bytes 5308416 | tf_op jit(solution)/shard_map/all_gather | solution.py:141
  264.0 58.2 %all-to-all-start.1 = ((bf16[288,8,720]{2,0,1:T(8,128)(2,1)}), bf16[288,8,720]{2,0,1:T(8,128)(2,1)}, u32[]{:S(2)}, u32[]{:S(2)}) async-start(bf16[288,8,720]{2,0,1:T(8,128)(2,1)} %copy.63), calls=%async_computation.1 | async-start | bytes 7077888 | tf_op jit(solution)/shard_map/all_to_all | solution.py:65
  322.2 46.6 %all-to-all-start.2 = ((bf16[288,8,720]{2,0,1:T(8,128)(2,1)}), bf16[288,8,720]{2,0,1:T(8,128)(2,1)}, u32[]{:S(2)}, u32[]{:S(2)}) async-start(bf16[288,8,720]{2,0,1:T(8,128)(2,1)} %copy.64), calls=%async_computation.2 | async-start | bytes 7077888 | tf_op jit(solution)/shard_map/all_to_all | solution.py:68
  344.6 28.7 %copy-start.12 = (s32[1,1024,2]{1,2,0:T(2,128)S(1)}, s32[1,1024,2]{1,2,0:T(2,128)}, u32[]{:S(2)}) copy-start(s32[1,1024,2]{1,2,0:T(2,128)} %param.15) | copy-start | bytes 24580
  368.8 46.6 %all-to-all-start.3 = ((bf16[288,8,720]{2,0,1:T(8,128)(2,1)}), bf16[288,8,720]{2,0,1:T(8,128)(2,1)}, u32[]{:S(2)}, u32[]{:S(2)}) async-start(bf16[288,8,720]{2,0,1:T(8,128)(2,1)} %copy.65), calls=%async_computation.3 | async-start | bytes 7077888 | tf_op jit(solution)/shard_map/all_to_all | solution.py:71
  373.3 124.9 %reduce-scatter.5.cloned.1.call-start = ((), (), s32[]{:S(2)}) async-start(), calls=%async_computation.11 | async-start | bytes 5308416 | tf_op jit(solution)/shard_map/reduce_scatter | solution.py:163
  457.3 5.7 %copy-start.6 = (bf16[1024,4,32]{0,2,1:T(8,128)(2,1)S(1)}, bf16[1024,4,32]{0,2,1:T(8,128)(2,1)}, u32[]{:S(2)}) copy-start(bf16[1024,4,32]{0,2,1:T(8,128)(2,1)} %copy-done.5) | copy-start | bytes 786436
  457.3 5.7 %copy-start.8 = (bf16[1024,4,32]{0,2,1:T(8,128)(2,1)S(1)}, bf16[1024,4,32]{0,2,1:T(8,128)(2,1)}, u32[]{:S(2)}) copy-start(bf16[1024,4,32]{0,2,1:T(8,128)(2,1)} %copy-done.7) | copy-start | bytes 786436
  463.1 3.4 copy-start.2
  463.1 35.1 %copy-start.3 = (bf16[128,2304]{1,0:T(8,128)(2,1)S(1)}, bf16[128,2304]{1,0:T(8,128)(2,1)}, u32[]{:S(2)}) copy-start(bf16[128,2304]{1,0:T(8,128)(2,1)} %reduce-scatter.3.cloned.1.call-done) | copy-start | bytes 1769476
  463.1 37.3 %copy-start.4 = (bf16[256,2304]{1,0:T(8,128)(2,1)S(1)}, bf16[256,2304]{1,0:T(8,128)(2,1)}, u32[]{:S(2)}) copy-start(bf16[256,2304]{1,0:T(8,128)(2,1)} %all-gather.7.cloned.1.call-done) | copy-start | bytes 3538948
Sparse Core Ops, SparseCore 0:
  42.0 69.6 all-gather.4
  114.2 37.5 all-gather.8
  153.9 30.4 all-gather.6
  189.4 52.9 reduce-scatter.2
  246.1 60.3 all-gather.10
  445.1 53.0 reduce-scatter.4
where the time goes:
time: 513 us; the launch traced here: 509 us
  waiting for transfers between devices  279 us (54%)
  local copies, waits for them, and re-layouts  91.6 us (18%)
  other arithmetic  47.8 us (9%)
  matrix products  40.3 us (8%)
  blocking collectives  18.9 us (4%)
  between operations  16 us (3%)
  starting transfers between devices  14.5 us (3%)
    all_gather x1, waiting for transfers between devices, shards(): lax.all_gather(column_part, 'dp', axis=0, tiled=True)  65.7 us
    reduce_scatter x1, waiting for transfers between devices, shards(): lax.psum_scatter(jnp.dot(attended, server_out, preferred_element_type=jnp...  52.6 us
    all_gather x1, waiting for transfers between devices, shards(): piece = lax.all_gather(normed, 'tensor', axis=0, tiled=True)  35.8 us
    all_to_all x1, waiting for transfers between devices, shards(): lax.all_to_all(trainer_gate.astype(jnp.bfloat16), 'tensor', split_axis=1,...  35.8 us
    reduce_scatter x1, waiting for transfers between devices, shards(): lax.psum_scatter(terms.astype(jnp.bfloat16), 'tensor', scatter_dimension=...  31.4 us
    unnamed x35, local copies, waits for them, and re-layouts  30.7 us
    all_to_all x1, waiting for transfers between devices, shards(): lax.all_to_all(trainer_up.astype(jnp.bfloat16), 'tensor', split_axis=1, c...  24.2 us
    all_to_all x1, waiting for transfers between devices, shards(): lax.all_to_all(trainer_down.astype(jnp.bfloat16), 'tensor', split_axis=1,...  24 us
  transfers between devices with their start and end apart: 9, of which 8 were waited for; matrix products, arithmetic and copies ran while one was open for 19% of the time, Pallas kernels for 0%

commit v1 on v0

--- a/solution.py
+++ b/solution.py
@@ -95,7 +95,13 @@
     normed = rms_scale(tokens, attn_gain).astype(jnp.bfloat16)
     local_width = server_qkv.shape[2]
     heads_here = local_width // HEAD_DIM
-    piece = lax.all_gather(normed, "tensor", axis=0, tiled=True)
+    count = lax.axis_size("tensor")
+    block, pieces = (normed, [normed])
+    for _ in range(count - 1):
+        block = lax.ppermute(block, "tensor", [(i, (i + 1) % count) for i in range(count)])
+        pieces.insert(0, block)
+    line = jnp.concatenate(pieces, axis=0)
+    piece = jnp.roll(line, (lax.axis_index("tensor") + 1) * normed.shape[0], axis=0)
     mixed = jnp.einsum("sd,dtc->stc", piece, server_qkv, preferred_element_type=jnp.float32)
     places = offset + jnp.arange(piece.shape[0], dtype=jnp.int32)
     query_rot = rotate(mixed[:, 0].reshape(-1, heads_here, HEAD_DIM), places).reshape(

time: 513 us -> 492 us (0.959)
  waiting for transfers between devices: 279 us -> 235 us
  local copies, waits for them, and re-layouts: 91.6 us -> 110 us
    ppermute x0 -> x7, waiting for transfers between devices: none -> 66.4 us  [shards(): lax.ppermute(block, 'tensor', [(i, (i + 1) % count) for i in range(count)])]
    all_gather x1, waiting for transfers between devices: 65.7 us -> 0.01 us  [shards(): lax.all_gather(column_part, 'dp', axis=0, tiled=True)]
    all_gather x1 -> x0, waiting for transfers between devices: 35.8 us -> none  [shards(): piece = lax.all_gather(normed, 'tensor', axis=0, tiled=True)]
    unnamed x35 -> x59, local copies, waits for them, and re-layouts: 30.7 us -> 49.7 us
    all_gather x1, waiting for transfers between devices: 9.96 us -> 0.02 us  [shards(): lax.all_gather(out_cast, 'dp', axis=0, tiled=True)]
  transfers between devices with their start and end apart: 9 -> 15, of which waited for: 8 -> 12; matrix products, arithmetic and copies ran while one was open for 19% -> 24% of each run, Pallas kernels for 0% -> 0%
where the time goes in v1:
time: 492 us; the launch traced here: 487 us
  waiting for transfers between devices  235 us (48%)
  local copies, waits for them, and re-layouts  110 us (22%)
  other arithmetic  52.3 us (11%)
  matrix products  40.5 us (8%)
  blocking collectives  18.9 us (4%)
  between operations  15.7 us (3%)
  starting transfers between devices  14.5 us (3%)
    ppermute x7, waiting for transfers between devices, shards(): lax.ppermute(block, 'tensor', [(i, (i + 1) % count) for i in range(count)])  66.4 us
    reduce_scatter x1, waiting for transfers between devices, shards(): lax.psum_scatter(jnp.dot(attended, server_out, preferred_element_type=jnp...  53.2 us
    unnamed x59, local copies, waits for them, and re-layouts  49.7 us
    all_to_all x1, waiting for transfers between devices, shards(): lax.all_to_all(trainer_gate.astype(jnp.bfloat16), 'tensor', split_axis=1,...  35.8 us
    reduce_scatter x1, waiting for transfers between devices, shards(): lax.psum_scatter(terms.astype(jnp.bfloat16), 'tensor', scatter_dimension=...  31.4 us
    all_to_all x1, waiting for transfers between devices, shards(): lax.all_to_all(trainer_up.astype(jnp.bfloat16), 'tensor', split_axis=1, c...  24.2 us
    all_to_all x1, waiting for transfers between devices, shards(): lax.all_to_all(trainer_down.astype(jnp.bfloat16), 'tensor', split_axis=1,...  24 us
    all_to_all x1, blocking collectives, shards(): lax.all_to_all(qkv_cast, 'tensor', split_axis=2, concat_axis=0, tiled=True)  18.9 us
  transfers between devices with their start and end apart: 15, of which 12 were waited for; matrix products, arithmetic and copies ran while one was open for 24% of the time, Pallas kernels for 0%

profile of v1, /device:TPU:0, one launch (start us, length us, event | category | flops | bytes accessed | tf_op | source)
XLA Modules:
  0.0 486.5 jit_solution(11267279683598034004)
XLA Ops:
  16.3 18.9 %all_to_all.75 = bf16[8,2,27648]{2,1,0:T(2,128)(2,1)} all-to-all(bf16[8,2,27648]{2,1,0:T(2,128)(2,1)} %reshape.272), channel_id=1, replica_groups=mesh['dp'=4,'tensor'=8] {'tensor'}, dimensions={0} | all-to-all | bytes 1769472 | tf_op jit(solution)/shard_map/all_to_all | solution.py:78
  42.5 10.2 %collective-permute-done = bf16[128,2304]{1,0:T(8,128)(2,1)S(1)} collective-permute-done((bf16[128,2304]{1,0:T(8,128)(2,1)S(1)}, bf16[128,2304]{1,0:T(8,128)(2,1)S(1)}, u32[]{:S(2)}, u32[]{:S(2)}) %collective-permute-start) | collective-permute-done | bytes 589856 | tf_op jit(solution)/shard_map/ppermute | solution.py:101
  52.7 10.2 %collective-permute-done.1 = bf16[128,2304]{1,0:T(8,128)(2,1)S(1)} collective-permute-done((bf16[128,2304]{1,0:T(8,128)(2,1)S(1)}, bf16[128,2304]{1,0:T(8,128)(2,1)S(1)}, u32[]{:S(2)}, u32[]{:S(2)}) %collective-permute-start.1) | collective-permute-done | bytes 589856 | tf_op jit(solution)/shard_map/ppermute | solution.py:101
  62.9 10.2 %collective-permute-done.2 = bf16[128,2304]{1,0:T(8,128)(2,1)S(1)} collective-permute-done((bf16[128,2304]{1,0:T(8,128)(2,1)S(1)}, bf16[128,2304]{1,0:T(8,128)(2,1)S(1)}, u32[]{:S(2)}, u32[]{:S(2)}) %collective-permute-start.2) | collective-permute-done | bytes 589856 | tf_op jit(solution)/shard_map/ppermute | solution.py:101
  73.1 10.2 %collective-permute-done.3 = bf16[128,2304]{1,0:T(8,128)(2,1)S(1)} collective-permute-done((bf16[128,2304]{1,0:T(8,128)(2,1)S(1)}, bf16[128,2304]{1,0:T(8,128)(2,1)S(1)}, u32[]{:S(2)}, u32[]{:S(2)}) %collective-permute-start.3) | collective-permute-done | bytes 589856 | tf_op jit(solution)/shard_map/ppermute | solution.py:101
  83.3 10.3 %collective-permute-done.4 = bf16[128,2304]{1,0:T(8,128)(2,1)} collective-permute-done((bf16[128,2304]{1,0:T(8,128)(2,1)S(1)}, bf16[128,2304]{1,0:T(8,128)(2,1)}, u32[]{:S(2)}, u32[]{:S(2)}) %collective-permute-start.4) | collective-permute-done | bytes 589856 | tf_op jit(solution)/shard_map/ppermute | solution.py:101
  96.1 8.0 %collective-permute-done.5 = bf16[128,2304]{1,0:T(8,128)(2,1)} collective-permute-done((bf16[128,2304]{1,0:T(8,128)(2,1)}, bf16[128,2304]{1,0:T(8,128)(2,1)}, u32[]{:S(2)}, u32[]{:S(2)}) %collective-permute-start.5) | collective-permute-done | bytes 589856 | tf_op jit(solution)/shard_map/ppermute | solution.py:101
  107.6 7.3 %collective-permute-done.6 = bf16[128,2304]{1,0:T(8,128)(2,1)} collective-permute-done((bf16[128,2304]{1,0:T(8,128)(2,1)}, bf16[128,2304]{1,0:T(8,128)(2,1)}, u32[]{:S(2)}, u32[]{:S(2)}) %collective-permute-start.6) | collective-permute-done | bytes 589856 | tf_op jit(solution)/shard_map/ppermute | solution.py:101
  138.0 7.1 %fusion.63 = (bf16[1024,3,256]{0,2,1:T(8,128)(2,1)S(1)}, f32[1024,3,256]{0,2,1:T(8,128)S(1)}) fusion(bf16[2304,3,256]{2,0,1:T(8,128)(2,1)S(1)} %bitcast.106, bf16[2048,2304]{1,0:T(8,128)(2,1)} %constant_dynamic-update-slice_fusion, s32[]{:T(128)S(6)} %select_n.80), kind=kOutput, calls=%fused_computation.126 | convolution fusion | flops 3624665088 | bytes 12976132 | tf_op jit(solution)/shard_map/sd,dtc->stc/dot_general | solution.py:105
  167.5 53.2 %reduce-scatter.3.cloned.1.call-done = bf16[128,2304]{1,0:T(8,128)(2,1)} async-done(((bf16[1024,2304]{1,0:T(8,128)(2,1)}), bf16[128,2304]{1,0:T(8,128)(2,1)}) %reduce-scatter.3.cloned.1.call-update) | async-done | bytes 589840 | tf_op jit(solution)/shard_map/reduce_scatter | solution.py:126
  229.2 8.5 %all_to_all.59 = bf16[288,8,720]{2,1,0:T(8,128)(2,1)} reshape(bf16[288,5760]{1,0:T(8,128)(2,1)} %convert_element_type.88) | data formatting | bytes 6635520 | tf_op jit(solution)/shard_map/all_to_all | solution.py:65
  251.8 8.5 %all_to_all.63 = bf16[288,8,720]{2,1,0:T(8,128)(2,1)} reshape(bf16[288,5760]{1,0:T(8,128)(2,1)} %convert_element_type.89) | data formatting | bytes 6635520 | tf_op jit(solution)/shard_map/all_to_all | solution.py:68
  264.7 35.8 %all-to-all-done.1 = bf16[288,8,720]{2,0,1:T(8,128)(2,1)} async-done(((bf16[288,8,720]{2,0,1:T(8,128)(2,1)}), bf16[288,8,720]{2,0,1:T(8,128)(2,1)}, u32[]{:S(2)}, u32[]{:S(2)}) %all-to-all-start.1) | async-done | bytes 3317792 | tf_op jit(solution)/shard_map/all_to_all | solution.py:65
  310.0 8.5 %all_to_all.67 = bf16[288,8,720]{2,1,0:T(8,128)(2,1)} reshape(bf16[288,5760]{1,0:T(8,128)(2,1)} %convert_element_type.90) | data formatting | bytes 6635520 | tf_op jit(solution)/shard_map/all_to_all | solution.py:71
  323.0 24.2 %all-to-all-done.2 = bf16[288,8,720]{2,0,1:T(8,128)(2,1)} async-done(((bf16[288,8,720]{2,0,1:T(8,128)(2,1)}), bf16[288,8,720]{2,0,1:T(8,128)(2,1)}, u32[]{:S(2)}, u32[]{:S(2)}) %all-to-all-start.2) | async-done | bytes 3317792 | tf_op jit(solution)/shard_map/all_to_all | solution.py:68
  356.9 7.8 %gather_fusion = bf16[512,2304]{1,0:T(8,128)(2,1)S(1)} fusion(bf16[1024,2304]{1,0:T(8,128)(2,1)} %all-gather.8.cloned.1.call-done, s32[1024]{0:T(1024)S(1)} %pad_clamp_fusion), kind=kCustom, calls=%fused_computation | custom fusion | bytes 4720640 | tf_op jit(solution)/shard_map/gather | solution.py:157
  369.8 24.0 %all-to-all-done.3 = bf16[288,8,720]{2,0,1:T(8,128)(2,1)} async-done(((bf16[288,8,720]{2,0,1:T(8,128)(2,1)}), bf16[288,8,720]{2,0,1:T(8,128)(2,1)}, u32[]{:S(2)}, u32[]{:S(2)}) %all-to-all-start.3) | async-done | bytes 3317792 | tf_op jit(solution)/shard_map/all_to_all | solution.py:71
  393.7 9.9 %fusion.33 = f32[512,2304]{1,0:T(8,128)} fusion(bf16[2304,720]{1,0:T(8,128)(2,1)} %bitcast.12, f32[512,720]{0,1:T(8,128)} %fusion.74, bf16[512,2304]{1,0:T(8,128)(2,1)S(1)} %gather_fusion, bf16[2304,720]{1,0:T(8,128)(2,1)} %bitcast.10), kind=kOutput, calls=%fused_computation.52 | convolution fusion | flops 3399598080 | bytes 15187968 | tf_op jit(solution)/shard_map/dot_general | solution.py:161
  403.7 13.3 %scatter_custom_fusion.1 = f32[1024,2304]{1,0:T(8,128)} fusion(s32[512]{0:T(512)S(1)} %get-tuple-element.57, f32[512,2304]{1,0:T(8,128)} %fusion.33, f32[]{:T(128)} %constant.23.clone.1), kind=kCustom, calls=%fused_computation.12 | custom fusion | flops 1179648 | bytes 9437696 | tf_op jit(solution)/shard_map/scatter-add | solution.py:167
  416.9 6.4 %convert_element_type.109 = bf16[1024,2304]{1,0:T(8,128)(2,1)} convert(f32[1024,2304]{1,0:T(8,128)} %scatter_custom_fusion.1) | non-fusion elementwise | flops 2359296 | bytes 14155776 | tf_op jit(solution)/shard_map/convert_element_type | solution.py:170
  424.1 5.7 %copy.68 = bf16[2304,720]{0,1:T(8,128)(2,1)} copy(bf16[2304,720]{1,0:T(8,128)(2,1)} %bitcast.8) | data formatting | bytes 6635520
  429.7 5.9 %copy.69 = bf16[2304,720]{0,1:T(8,128)(2,1)} copy(bf16[2304,720]{1,0:T(8,128)(2,1)} %bitcast.10) | data formatting | bytes 6635520
  435.7 5.7 %copy.70 = bf16[2304,720]{0,1:T(8,128)(2,1)} copy(bf16[2304,720]{1,0:T(8,128)(2,1)} %bitcast.12) | data formatting | bytes 6635520
  445.1 31.4 %reduce-scatter.5.cloned.1.call-done = bf16[128,2304]{1,0:T(8,128)(2,1)} async-done(((bf16[1024,2304]{1,0:T(8,128)(2,1)}), bf16[128,2304]{1,0:T(8,128)(2,1)}) %reduce-scatter.5.cloned.1.call-update) | async-done | bytes 589840 | tf_op jit(solution)/shard_map/reduce_scatter | solution.py:169
  (136 shorter events, 129.7 us)
Async XLA Ops:
  7.2 437.7 %copy-start = (bf16[2304,8]{0,1:T(8,128)(2,1)S(1)}, bf16[2304,8]{0,1:T(8,128)(2,1)}, u32[]{:S(2)}) copy-start(bf16[2304,8]{0,1:T(8,128)(2,1)} %param.23) | copy-start | bytes 110596
  7.2 128.3 %all-gather.4.cloned.1.call-start = ((), (), s32[]{:S(2)}) async-start(), calls=%async_computation.6 | async-start | bytes 4423680 | tf_op jit(solution)/shard_map/all_gather | solution.py:80
  35.2 6.7 %copy-start.1 = (bf16[1,128,2304]{2,1,0:T(8,128)(2,1)S(1)}, bf16[1,128,2304]{2,1,0:T(8,128)(2,1)}, u32[]{:S(2)}) copy-start(bf16[1,128,2304]{2,1,0:T(8,128)(2,1)} %param.12) | copy-start | bytes 1769476
  35.2 7.0 %copy-start.15 = (f32[2304]{0:T(1024)S(1)}, f32[2304]{0:T(1024)}, u32[]{:S(2)}) copy-start(f32[2304]{0:T(1024)} %param.21) | copy-start | bytes 27652
  41.9 120.2 %all-gather.6.cloned.1.call-start = ((), (), s32[]{:S(2)}) async-start(), calls=%async_computation.7 | async-start | bytes 1474560 | tf_op jit(solution)/shard_map/all_gather | solution.py:81
  42.4 10.3 %collective-permute-start = (bf16[128,2304]{1,0:T(8,128)(2,1)S(1)}, bf16[128,2304]{1,0:T(8,128)(2,1)S(1)}, u32[]{:S(2)}, u32[]{:S(2)}) collective-permute-start(bf16[128,2304]{1,0:T(8,128)(2,1)S(1)} %fusion.26), channel_id=1, source_target_pairs={{0,1},{1,2},{2,3},{3,4},{4,5},{5,6},{6,7},{7,0},{8,9},{9,10},{10,1... | collective-permute-start | bytes 1769480 | tf_op jit(solution)/shard_map/ppermute | solution.py:101
  52.6 10.2 %collective-permute-start.1 = (bf16[128,2304]{1,0:T(8,128)(2,1)S(1)}, bf16[128,2304]{1,0:T(8,128)(2,1)S(1)}, u32[]{:S(2)}, u32[]{:S(2)}) collective-permute-start(bf16[128,2304]{1,0:T(8,128)(2,1)S(1)} %collective-permute-done), channel_id=1, source_target_pairs={{0,1},{1,2},{2,3},{3,4},{4,5},{5,6},{6,7},{7,0},{8,9},{9,10},{10,1... | collective-permute-start | bytes 1769480 | tf_op jit(solution)/shard_map/ppermute | solution.py:101
  62.9 10.2 %collective-permute-start.2 = (bf16[128,2304]{1,0:T(8,128)(2,1)S(1)}, bf16[128,2304]{1,0:T(8,128)(2,1)S(1)}, u32[]{:S(2)}, u32[]{:S(2)}) collective-permute-start(bf16[128,2304]{1,0:T(8,128)(2,1)S(1)} %collective-permute-done.1), channel_id=1, source_target_pairs={{0,1},{1,2},{2,3},{3,4},{4,5},{5,6},{6,7},{7,0},{8,9},{9,10},{10,1... | collective-permute-start | bytes 1769480 | tf_op jit(solution)/shard_map/ppermute | solution.py:101
  73.1 10.2 %collective-permute-start.3 = (bf16[128,2304]{1,0:T(8,128)(2,1)S(1)}, bf16[128,2304]{1,0:T(8,128)(2,1)S(1)}, u32[]{:S(2)}, u32[]{:S(2)}) collective-permute-start(bf16[128,2304]{1,0:T(8,128)(2,1)S(1)} %collective-permute-done.2), channel_id=1, source_target_pairs={{0,1},{1,2},{2,3},{3,4},{4,5},{5,6},{6,7},{7,0},{8,9},{9,10},{10,1... | collective-permute-start | bytes 1769480 | tf_op jit(solution)/shard_map/ppermute | solution.py:101
  83.3 10.3 %collective-permute-start.4 = (bf16[128,2304]{1,0:T(8,128)(2,1)S(1)}, bf16[128,2304]{1,0:T(8,128)(2,1)}, u32[]{:S(2)}, u32[]{:S(2)}) collective-permute-start(bf16[128,2304]{1,0:T(8,128)(2,1)S(1)} %collective-permute-done.3), channel_id=1, source_target_pairs={{0,1},{1,2},{2,3},{3,4},{4,5},{5,6},{6,7},{7,0},{8,9},{9,10},{10,1... | collective-permute-start | bytes 1769480 | tf_op jit(solution)/shard_map/ppermute | solution.py:101
  93.6 10.5 %collective-permute-start.5 = (bf16[128,2304]{1,0:T(8,128)(2,1)}, bf16[128,2304]{1,0:T(8,128)(2,1)}, u32[]{:S(2)}, u32[]{:S(2)}) collective-permute-start(bf16[128,2304]{1,0:T(8,128)(2,1)} %collective-permute-done.4), channel_id=1, source_target_pairs={{0,1},{1,2},{2,3},{3,4},{4,5},{5,6},{6,7},{7,0},{8,9},{9,10},{10,1... | collective-permute-start | bytes 1769480 | tf_op jit(solution)/shard_map/ppermute | solution.py:101
  95.4 125.3 %reduce-scatter.3.cloned.1.call-start = ((), (), s32[]{:S(2)}) async-start(), calls=%async_computation.8 | async-start | bytes 5308416 | tf_op jit(solution)/shard_map/reduce_scatter | solution.py:126
  104.1 10.8 %collective-permute-start.6 = (bf16[128,2304]{1,0:T(8,128)(2,1)}, bf16[128,2304]{1,0:T(8,128)(2,1)}, u32[]{:S(2)}, u32[]{:S(2)}) collective-permute-start(bf16[128,2304]{1,0:T(8,128)(2,1)} %collective-permute-done.5), channel_id=1, source_target_pairs={{0,1},{1,2},{2,3},{3,4},{4,5},{5,6},{6,7},{7,0},{8,9},{9,10},{10,1... | collective-permute-start | bytes 1769480 | tf_op jit(solution)/shard_map/ppermute | solution.py:101
  137.9 7.1 %copy-start.5 = (bf16[8,4,72,3,256]{4,2,1,0,3:T(8,128)(2,1)}, bf16[8,4,72,3,256]{4,2,1,0,3:T(8,128)(2,1)S(1)}, u32[]{:S(2)}) copy-start(bf16[8,4,72,3,256]{4,2,1,0,3:T(8,128)(2,1)S(1)} %copy.62) | copy-start | bytes 10616836
  166.9 55.2 %copy-start.16 = (f32[2304]{0:T(1024)S(1)}, f32[2304]{0:T(1024)}, u32[]{:S(2)}) copy-start(f32[2304]{0:T(1024)} %param.22) | copy-start | bytes 27652
  167.0 189.9 %all-gather.8.cloned.1.call-start = ((), (), s32[]{:S(2)}) async-start(), calls=%async_computation.9 | async-start | bytes 5308416 | tf_op jit(solution)/shard_map/all_gather | solution.py:147
  242.3 58.2 %all-to-all-start.1 = ((bf16[288,8,720]{2,0,1:T(8,128)(2,1)}), bf16[288,8,720]{2,0,1:T(8,128)(2,1)}, u32[]{:S(2)}, u32[]{:S(2)}) async-start(bf16[288,8,720]{2,0,1:T(8,128)(2,1)} %copy.63), calls=%async_computation.1 | async-start | bytes 7077888 | tf_op jit(solution)/shard_map/all_to_all | solution.py:65
  300.5 46.6 %all-to-all-start.2 = ((bf16[288,8,720]{2,0,1:T(8,128)(2,1)}), bf16[288,8,720]{2,0,1:T(8,128)(2,1)}, u32[]{:S(2)}, u32[]{:S(2)}) async-start(bf16[288,8,720]{2,0,1:T(8,128)(2,1)} %copy.64), calls=%async_computation.2 | async-start | bytes 7077888 | tf_op jit(solution)/shard_map/all_to_all | solution.py:68
  323.0 28.7 %copy-start.17 = (s32[1,1024,2]{1,2,0:T(2,128)S(1)}, s32[1,1024,2]{1,2,0:T(2,128)}, u32[]{:S(2)}) copy-start(s32[1,1024,2]{1,2,0:T(2,128)} %param.15) | copy-start | bytes 24580
  347.1 46.6 %all-to-all-start.3 = ((bf16[288,8,720]{2,0,1:T(8,128)(2,1)}), bf16[288,8,720]{2,0,1:T(8,128)(2,1)}, u32[]{:S(2)}, u32[]{:S(2)}) async-start(bf16[288,8,720]{2,0,1:T(8,128)(2,1)} %copy.65), calls=%async_computation.3 | async-start | bytes 7077888 | tf_op jit(solution)/shard_map/all_to_all | solution.py:71
  351.6 124.9 %reduce-scatter.5.cloned.1.call-start = ((), (), s32[]{:S(2)}) async-start(), calls=%async_computation.10 | async-start | bytes 5308416 | tf_op jit(solution)/shard_map/reduce_scatter | solution.py:169
  435.7 5.7 %copy-start.9 = (bf16[1024,4,32]{0,2,1:T(8,128)(2,1)S(1)}, bf16[1024,4,32]{0,2,1:T(8,128)(2,1)}, u32[]{:S(2)}) copy-start(bf16[1024,4,32]{0,2,1:T(8,128)(2,1)} %copy-done.8) | copy-start | bytes 786436
  441.4 35.1 %copy-start.3 = (bf16[128,2304]{1,0:T(8,128)(2,1)S(1)}, bf16[128,2304]{1,0:T(8,128)(2,1)}, u32[]{:S(2)}) copy-start(bf16[128,2304]{1,0:T(8,128)(2,1)} %reduce-scatter.3.cloned.1.call-done) | copy-start | bytes 1769476
  441.5 37.3 %copy-start.4 = (bf16[256,2304]{1,0:T(8,128)(2,1)S(1)}, bf16[256,2304]{1,0:T(8,128)(2,1)}, u32[]{:S(2)}) copy-start(bf16[256,2304]{1,0:T(8,128)(2,1)} %all-gather.6.cloned.1.call-done) | copy-start | bytes 3538948
  (10 other events, 33.9 us)
Sparse Core Ops, SparseCore 0:
  42.0 69.6 all-gather.3
  113.9 29.0 all-gather.5
  167.1 53.6 reduce-scatter.2
  224.4 60.3 all-gather.7
  423.5 53.0 reduce-scatter.4
